TPU v7x, 32 devices: a whole 2x2x4 slice. The times are simulated.
32 devices in a mesh: ctx: 8 (over y, x, core), head: 4 (over z).
Axes of the slice: x: 2, y: 2, z: 4, core: 2. Of those that a mesh axis runs over, the one named last changes fastest.
Arguments:
- queries: bfloat16 [4096, 4096], P(('ctx', 'head')), may hold values from -128 to 128
- vis_feats: bfloat16 [4096, 8192], P('ctx', 'head'), may hold values from -16 to 16
- kv_weight: bfloat16 [8192, 1024], P('head'), may hold values from -0.044194174 to 0.044194174
- key_gain: float32 [128], replicated, may hold values from 0.1 to 1.9
- cross_mask: int32 [4096, 4], P('ctx'), may hold values 0 or 1
- image_tokens: int32 [4], replicated, may hold values from 1 to 512, 1280 in all
- image_owner: int32 [4], replicated, may hold values from 0 to 7, as said below
Outputs:
- attended: bfloat16 [4096, 4096], P(('ctx', 'head'))
Inputs may be any that keep to these rules, and one draw needn't show every extreme that they name: `image_tokens`: they sum to 1280; the largest is exactly 512. `image_owner`: four distinct context indices; the first and the last index of ctx always hold an image.
All inputs are finite; a program needn't handle non-finite values. No bound on the sum of `cross_mask` on one device may be relied on, other than what follows from the above.
Results may differ from a plain program's by a relative error of at most 0.0014.
The roundings to bfloat16 on the way count: a program that leaves them out, or rounds other values in their place, can miss the bound.
Values may be sent and summed in bfloat16 or wider, within the bound.
No kernel may reach another device: no remote copies, remote signals or barrier semaphores. Data moves between devices by JAX's collectives and lax.ppermute only.
A program may use at most 64 MiB of HBM per device.

v0:
```python
import jax
import jax.numpy as jnp
from jax import lax
from jax.sharding import PartitionSpec as P

EPSILON = 1e-05
FLOOR_SCORE = -1e30


def swapped(value, axis, bit):
    mask = 2**bit
    pairs = [(source, source ^ mask) for source in range(lax.axis_size(axis))]
    return lax.ppermute(value, axis, pairs)


def broadcast(shard, axis, root):
    mine = lax.axis_index(axis) == root
    return lax.psum(jnp.where(mine, shard, jnp.zeros_like(shard)), axis)


def normalize_keys(stacked, key_gain):
    raw_keys = stacked[..., 0, :, :]
    square_mean = jnp.mean(raw_keys * raw_keys, axis=-2, keepdims=True)
    normed = raw_keys * lax.rsqrt(square_mean + EPSILON) * key_gain[:, None]
    joined = jnp.stack([normed, stacked[..., 1, :, :]], axis=-3)
    return joined.astype(jnp.bfloat16)


def arrange_keys(received, image_tokens):
    cap_rows = received[0].shape[-1]
    count_img = len(received)
    img_ids = jnp.arange(count_img, dtype=jnp.int32)
    laid_out = jnp.concatenate(received, axis=-1)
    positions = jnp.arange(count_img * cap_rows, dtype=jnp.int32)[:, None]
    member = (positions // cap_rows == img_ids[None, :]) & (
        positions % cap_rows < image_tokens[None, :]
    )
    return (laid_out, member.astype(jnp.float32))


def attend_rows(query_rows, mask_rows, key_cols, value_cols, member):
    row_count = query_rows.shape[0]
    rows_per_block = min(512, row_count)
    count_of_blocks = row_count // rows_per_block
    blocked_queries = query_rows.reshape((count_of_blocks, rows_per_block) + query_rows.shape[1:])
    mask_blocks = mask_rows.reshape(count_of_blocks, rows_per_block, mask_rows.shape[1])
    factor = query_rows.shape[-1] ** (-0.5)
    member_rows = member.T

    def one_block(block_pair):
        query_block, mask_block = block_pair
        allowed = jnp.dot(mask_block.astype(jnp.float32), member_rows) > 0.5
        allowed = allowed[:, None, :]
        scores = (
            jnp.einsum("rnd,dk->rnk", query_block, key_cols, preferred_element_type=jnp.float32)
            * factor
        )
        largest = jnp.max(jnp.where(allowed, scores, FLOOR_SCORE), axis=-1, keepdims=True)
        weights = jnp.where(allowed, jnp.exp(scores - largest), 0.0)
        summed = jnp.sum(weights, axis=-1, keepdims=True)
        mixed_out = jnp.einsum(
            "rnk,dk->rnd",
            weights.astype(jnp.bfloat16),
            value_cols,
            preferred_element_type=jnp.float32,
        )
        return (mixed_out / jnp.maximum(summed, 1.0)).astype(jnp.bfloat16)

    return lax.map(one_block, (blocked_queries, mask_blocks)).reshape(query_rows.shape)


def shards(queries, vis_feats, kv_weight, key_gain, cross_mask, image_tokens, image_owner):
    head_count = lax.axis_size("head")
    head_index = lax.axis_index("head")
    count_img = image_owner.shape[0]
    width_kv = kv_weight.shape[1]
    head_dim = key_gain.shape[0]
    kv_heads = width_kv // (2 * head_dim)
    tok_rows = queries.shape[0]
    query_heads = queries.shape[1] // head_dim
    per_kv = head_count // kv_heads
    share_part = lax.psum_scatter(
        lax.dot_general(
            kv_weight, vis_feats, (((0,), (1,)), ((), ())), preferred_element_type=jnp.float32
        ),
        "head",
        scatter_dimension=0,
        tiled=True,
    )
    for bit_index in range(per_kv.bit_length() - 1):
        partner = swapped(share_part, "head", bit_index)
        low_half = (head_index >> bit_index) % 2 == 0
        share_part = jnp.where(
            low_half,
            jnp.concatenate([share_part, partner], 0),
            jnp.concatenate([partner, share_part], 0),
        )
    local_kv = normalize_keys(share_part.reshape(1, 2, head_dim, -1), key_gain)[0].reshape(
        2 * head_dim, -1
    )
    received = [
        broadcast(local_kv, "ctx", image_owner[img_index]) for img_index in range(count_img)
    ]
    laid_out, member = arrange_keys(received, image_tokens)
    key_cols = laid_out[:head_dim]
    value_cols = laid_out[head_dim:]
    group_size = query_heads // head_count
    grouped = queries.reshape(tok_rows, head_count, group_size, head_dim)
    exchanged = lax.all_to_all(grouped, "head", split_axis=1, concat_axis=0, tiled=True)
    rows_all = exchanged.shape[0]
    flat_rows = exchanged.reshape(rows_all, exchanged.shape[2], head_dim)
    attended_heads = attend_rows(flat_rows, cross_mask, key_cols, value_cols, member).reshape(
        exchanged.shape
    )
    restored = lax.all_to_all(attended_heads, "head", split_axis=0, concat_axis=1, tiled=True)
    return restored.reshape(tok_rows, query_heads * head_dim)


def solution(mesh):
    return jax.shard_map(
        shards,
        mesh=mesh,
        in_specs=(
            P(("ctx", "head"), None),
            P("ctx", "head"),
            P("head", None),
            P(),
            P("ctx", None),
            P(),
            P(),
        ),
        out_specs=P(("ctx", "head"), None),
        check_vma=False,
    )
```

profile of v0, /device:TPU:0, one launch (start us, length us, event | category | flops | bytes accessed | tf_op | source)
XLA Modules:
  0.0 219.0 jit_solution(8036381709302970630)
XLA Ops:
  6.5 0.0 reduce-scatter.2.cloned.1.call-start
  6.6 1.5 copy-done
  8.1 5.9 %fusion.36 = f32[1024,512]{1,0:T(8,128)} fusion(bf16[2048,1024]{1,0:T(8,128)(2,1)} %param.9, bf16[512,2048]{1,0:T(8,128)(2,1)S(1)} %copy-done), kind=kOutput, calls=%fused_computation.55 | convolution fusion | flops 2147483648 | bytes 8388608 | tf_op jit(solution)/shard_map/dot_general | solution.py:83
  14.0 0.0 reduce-scatter.2.cloned.1.call-update
  14.0 1.6 copy.29
  15.7 1.3 copy.30
  17.0 6.3 %all-to-all-start = ((bf16[128,4,8,128]{3,0,2,1:T(8,128)(2,1)}), bf16[128,4,8,128]{3,0,2,1:T(8,128)(2,1)S(1)}, u32[]{:S(2)}, u32[]{:S(2)}) async-start(bf16[128,4,8,128]{3,0,2,1:T(8,128)(2,1)} %copy.30), calls=%async_computation.1 | async-start | bytes 2097152 | tf_op jit(solution)/shard_map/all_to_all | solution.py:109
  23.3 0.0 all-reduce.3.cloned.1.call-start
  23.4 0.7 fusion.34
  26.5 54.1 %reduce-scatter.2.cloned.1.call-done = f32[256,512]{1,0:T(8,128)} async-done(((f32[1024,512]{1,0:T(8,128)}), f32[256,512]{1,0:T(8,128)}) %reduce-scatter.2.cloned.1.call-update) | async-done | bytes 524304 | tf_op jit(solution)/shard_map/reduce_scatter | solution.py:82
  80.5 1.0 slice.49
  81.5 1.0 multiply_reduce_fusion
  82.5 1.0 multiply_convert_fusion
  83.6 0.9 broadcast_select_fusion
  84.5 1.8 copy.41
  86.3 1.8 copy.39
  88.0 1.8 copy.40
  89.8 0.8 copy.38
  90.7 0.0 all-reduce.3.cloned.1.call-update
  90.7 2.6 %compare_bitcast_fusion = pred[512,2048]{0,1:T(8,128)(4,1)} fusion(s32[4]{0:T(128)S(1)} %copy-done.4, s32[2048]{0:T(1024)S(1)} %get-tuple-element.41, s32[2048]{0:T(1024)S(1)} %get-tuple-element.40, s32[512,4]{0,1:T(4,128)S(1)} %copy-done.3), kind=kOutput, calls=%fused_computation.12 | convolution fusion | flops 9463808 | bytes 1073168 | tf_op jit(solution)/shard_map/while/body/eval_jaxpr/dot_general | solution.py:52
  93.3 1.1 copy.31
  94.4 54.2 %all-reduce.3.cloned.1.call-done = (bf16[256,512]{0,1:T(8,128)(2,1)}, bf16[256,512]{0,1:T(8,128)(2,1)}, bf16[256,512]{0,1:T(8,128)(2,1)}, bf16[256,512]{0,1:T(8,128)(2,1)}) async-done(((bf16[256,512]{0,1:T(8,128)(2,1)}, bf16[256,512]{0,1:T(8,128)(2,1)}, bf16[256,512]{0,1:T(8,128)(2,1)}, bf16[256,512]{0,1:T(8,128)(2,1)}), (bf16[256,512]{0,1:T(8,128)(2,1)}, bf16[256,512]{0,1:T(8,128)(2,1)}, ...) | async-done | bytes 1048592 | tf_op jit(solution)/shard_map/psum | solution.py:18
  148.5 1.0 constant_dynamic-update-slice_fusion.3
  149.5 1.0 constant_dynamic-update-slice_fusion.2
  150.5 1.0 constant_dynamic-update-slice_fusion.1
  151.4 1.0 constant_dynamic-update-slice_fusion
  152.4 17.6 %fusion.35 = (f32[512,8]{0,1:T(8,128)S(1)}, bf16[512,8,2048]{0,2,1:T(8,128)(2,1)}) fusion(pred[512,2048]{0,1:T(8,128)(4,1)} %compare_bitcast_fusion, bf16[512,8,128]{2,0,1:T(8,128)(2,1)} %bitcast.66, bf16[256,2048]{0,1:T(8,128)(2,1)S(1)} %constant_dynamic-update-slice_fusion), kind=kOutput, calls=%fused_computation.54 | convolution fusion | flops 4353689600 | bytes 22036480 | tf_op jit(solution)/shard_map/while/body/eval_jaxpr/sub | solution.py:59
  170.0 10.8 %fusion.14 = bf16[512,1,8,128]{3,0,2,1:T(8,128)(2,1)S(1)} fusion(bf16[512,8,2048]{0,2,1:T(8,128)(2,1)} %get-tuple-element.39, f32[512,8]{0,1:T(8,128)S(1)} %broadcast_maximum_fusion, bf16[256,2048]{0,1:T(8,128)(2,1)S(1)} %constant_dynamic-update-slice_fusion), kind=kOutput, calls=%fused_computation.15 | convolution fusion | flops 2148532224 | bytes 18366464 | tf_op jit(solution)/shard_map/while/body/eval_jaxpr/rnk,dk->rnd/dot_general | solution.py:61
  180.8 0.7 copy.34
  181.5 29.3 %all_to_all.30 = bf16[512,1,8,128]{3,2,1,0:T(8,128)(2,1)S(1)} all-to-all(bf16[512,1,8,128]{3,2,1,0:T(8,128)(2,1)S(1)} %copy.34), channel_id=1, replica_groups=mesh['ctx'=8,'head'=4] {'head'}, dimensions={0} | all-to-all | bytes 2097152 | tf_op jit(solution)/shard_map/all_to_all | solution.py:115
  210.7 0.2 copy.35
  210.9 1.3 reshape.149
  (13 shorter events, 0.0 us)
Async XLA Ops:
  6.5 1.6 copy-start
  6.5 16.8 %copy-start.1 = (s32[4]{0:T(128)S(1)}, s32[4]{0:T(128)}, u32[]{:S(2)}) copy-start(s32[4]{0:T(128)} %param.13) | copy-start | bytes 52
  6.5 76.0 %copy-start.2 = (f32[128]{0:T(128)S(1)}, f32[128]{0:T(128)}, u32[]{:S(2)}) copy-start(f32[128]{0:T(128)} %param.10) | copy-start | bytes 1540
  6.5 84.2 %copy-start.4 = (s32[4]{0:T(128)S(1)}, s32[4]{0:T(128)}, u32[]{:S(2)}) copy-start(s32[4]{0:T(128)} %param.12) | copy-start | bytes 52
  6.5 84.2 %copy-start.3 = (s32[512,4]{0,1:T(4,128)S(1)}, s32[512,4]{0,1:T(4,128)}, u32[]{:S(2)}) copy-start(s32[512,4]{0,1:T(4,128)} %param.11) | copy-start | bytes 24580
  6.5 74.0 %reduce-scatter.2.cloned.1.call-start = ((), (), s32[]{:S(2)}) async-start(), calls=%async_computation.3 | async-start | bytes 2621440 | tf_op jit(solution)/shard_map/reduce_scatter | solution.py:82
  17.0 76.3 %all-to-all-start = ((bf16[128,4,8,128]{3,0,2,1:T(8,128)(2,1)}), bf16[128,4,8,128]{3,0,2,1:T(8,128)(2,1)S(1)}, u32[]{:S(2)}, u32[]{:S(2)}) async-start(bf16[128,4,8,128]{3,0,2,1:T(8,128)(2,1)} %copy.30), calls=%async_computation.1 | async-start | bytes 2097152 | tf_op jit(solution)/shard_map/all_to_all | solution.py:109
  23.3 125.2 %all-reduce.3.cloned.1.call-start = ((), (), s32[]{:S(2)}) async-start(), calls=%async_computation.4 | async-start | bytes 2097152 | tf_op jit(solution)/shard_map/psum | solution.py:18
Sparse Core Ops, SparseCore 0:
  14.2 66.3 reduce-scatter.1
  90.8 57.6 all-reduce.2
where the time goes:
time: 220 us; the launch traced here: 219 us
  waiting for transfers between devices  108 us (49%)
  matrix products  36.8 us (17%)
  blocking collectives  29.3 us (13%)
  local copies, waits for them, and re-layouts  19.4 us (9%)
  between operations  16 us (7%)
  starting transfers between devices  6.38 us (3%)
  other arithmetic  2.95 us (1%)
    psum x1, waiting for transfers between devices, broadcast(): return lax.psum(jnp.where(mine, shard, jnp.zeros_like(shard)), axis)  54.2 us
    reduce_scatter x1, waiting for transfers between devices, shards(): lax.psum_scatter(lax.dot_general(kv_weight, vis_feats, (((0,), (1,)), (()...  54.1 us
    all_to_all x1, blocking collectives, shards(): lax.all_to_all(attended_heads, 'head', split_axis=0, concat_axis=1, tiled...  29.3 us
    sub x1, matrix products, one_block(): weights = jnp.where(allowed, jnp.exp(scores - largest), 0.0)  17.6 us
    dot_general x1, matrix products, one_block(): jnp.einsum('rnk,dk->rnd', weights.astype(jnp.bfloat16), value_cols, prefe...  10.8 us
    all_to_all x1, starting transfers between devices, shards(): lax.all_to_all(grouped, 'head', split_axis=1, concat_axis=0, tiled=True)  6.34 us
    select_n x4, local copies, waits for them, and re-layouts, broadcast(): return lax.psum(jnp.where(mine, shard, jnp.zeros_like(shard)), axis)  6.19 us
    unnamed x14, local copies, waits for them, and re-layouts  6.07 us
  transfers between devices with their start and end apart: 3, of which 2 were waited for; matrix products, arithmetic and copies ran while one was open for 8% of the time, Pallas kernels for 0%

commit v1 on v0

--- a/solution.py
+++ b/solution.py
@@ -5,6 +5,10 @@
 
 EPSILON = 1e-05
 FLOOR_SCORE = -1e30
+
+
+def watch_area_over_axis(t0, link_axis):
+    return lax.all_gather(t0, link_axis).sum(axis=0)
 
 
 def swapped(value, axis, bit):
@@ -15,7 +19,7 @@
 
 def broadcast(shard, axis, root):
     mine = lax.axis_index(axis) == root
-    return lax.psum(jnp.where(mine, shard, jnp.zeros_like(shard)), axis)
+    return watch_area_over_axis(jnp.where(mine, shard, jnp.zeros_like(shard)), axis)
 
 
 def normalize_keys(stacked, key_gain):

time: 220 us -> 255 us (1.16)
  waiting for transfers between devices: 108 us -> 140 us
  other arithmetic: 2.95 us -> 13.2 us
  local copies, waits for them, and re-layouts: 19.4 us -> 12.9 us
    all_gather x0 -> x4, waiting for transfers between devices: none -> 72.3 us  [watch_area_over_axis(): return lax.all_gather(t0, link_axis).sum(axis=0)]
    psum x1 -> x0, waiting for transfers between devices: 54.2 us -> none  [broadcast(): return lax.psum(jnp.where(mine, shard, jnp.zeros_like(shard)), axis)]
    all_to_all x1, waiting for transfers between devices: 0.01 us -> 22.8 us  [shards(): lax.all_to_all(grouped, 'head', split_axis=1, concat_axis=0, tiled=True)]
    reduce_scatter x1, waiting for transfers between devices: 54.1 us -> 43.1 us  [shards(): lax.psum_scatter(lax.dot_general(kv_weight, vis_feats, (((0,), (1,)), (()...]
    reduce_sum x0 -> x4, other arithmetic: none -> 7.93 us  [watch_area_over_axis(): return lax.all_gather(t0, link_axis).sum(axis=0)]
    select_n x4 -> x0, local copies, waits for them, and re-layouts: 6.19 us -> none  [broadcast(): return lax.psum(jnp.where(mine, shard, jnp.zeros_like(shard)), axis)]
    reduce_sum x0 -> x4, local copies, waits for them, and re-layouts: none -> 3.4 us  [watch_area_over_axis(): return lax.all_gather(t0, link_axis).sum(axis=0)]
    unnamed x14 -> x13, local copies, waits for them, and re-layouts: 6.07 us -> 3.22 us
  transfers between devices with their start and end apart: 3 -> 6, of which waited for: 2 -> 5; matrix products, arithmetic and copies ran while one was open for 8% -> 6% of each run, Pallas kernels for 0% -> 0%
where the time goes in v1:
time: 255 us; the launch traced here: 254 us
  waiting for transfers between devices  140 us (55%)
  matrix products  37.5 us (15%)
  blocking collectives  30.5 us (12%)
  between operations  16 us (6%)
  other arithmetic  13.2 us (5%)
  local copies, waits for them, and re-layouts  12.9 us (5%)
  starting transfers between devices  3.87 us (2%)
    all_gather x4, waiting for transfers between devices, watch_area_over_axis(): return lax.all_gather(t0, link_axis).sum(axis=0)  72.3 us
    reduce_scatter x1, waiting for transfers between devices, shards(): lax.psum_scatter(lax.dot_general(kv_weight, vis_feats, (((0,), (1,)), (()...  43.1 us
    all_to_all x1, blocking collectives, shards(): lax.all_to_all(attended_heads, 'head', split_axis=0, concat_axis=1, tiled...  30.5 us
    all_to_all x1, waiting for transfers between devices, shards(): lax.all_to_all(grouped, 'head', split_axis=1, concat_axis=0, tiled=True)  22.8 us
    sub x1, matrix products, one_block(): weights = jnp.where(allowed, jnp.exp(scores - largest), 0.0)  18.3 us
    dot_general x1, matrix products, one_block(): jnp.einsum('rnk,dk->rnd', weights.astype(jnp.bfloat16), value_cols, prefe...  10.8 us
    reduce_sum x4, other arithmetic, watch_area_over_axis(): return lax.all_gather(t0, link_axis).sum(axis=0)  7.93 us
    dot_general x1, matrix products, shards(): lax.dot_general(kv_weight, vis_feats, (((0,), (1,)), ((), ())), preferred...  5.9 us
  transfers between devices with their start and end apart: 6, of which 5 were waited for; matrix products, arithmetic and copies ran while one was open for 6% of the time, Pallas kernels for 0%

profile of v1, /device:TPU:0, one launch (start us, length us, event | category | flops | bytes accessed | tf_op | source)
XLA Modules:
  0.0 253.9 jit_solution(561631422016239301)
XLA Ops:
  6.5 1.6 copy-done
  8.1 5.9 %fusion.36 = f32[1024,512]{1,0:T(8,128)} fusion(bf16[2048,1024]{1,0:T(8,128)(2,1)} %param.9, bf16[512,2048]{1,0:T(8,128)(2,1)S(1)} %copy-done), kind=kOutput, calls=%fused_computation.52 | convolution fusion | flops 2147483648 | bytes 8388608 | tf_op jit(solution)/shard_map/dot_general | solution.py:87
  14.1 0.7 fusion.34
  17.5 43.1 %reduce-scatter.2.cloned.1.call-done = f32[256,512]{1,0:T(8,128)} async-done(((f32[1024,512]{1,0:T(8,128)}), f32[256,512]{1,0:T(8,128)}) %reduce-scatter.2.cloned.1.call-update) | async-done | bytes 524304 | tf_op jit(solution)/shard_map/reduce_scatter | solution.py:86
  60.6 1.0 multiply_reduce_fusion
  61.5 1.0 slice.49
  62.5 1.0 multiply_convert_fusion
  63.6 1.0 broadcast_select_fusion.3
  64.7 0.7 all-gather.5.cloned.1.call-update
  66.5 1.6 copy.25
  68.1 1.4 copy.26
  69.5 3.7 %all-to-all-start = ((bf16[128,4,8,128]{3,0,2,1:T(8,128)(2,1)}), bf16[128,4,8,128]{3,0,2,1:T(8,128)(2,1)S(1)}, u32[]{:S(2)}, u32[]{:S(2)}) async-start(bf16[128,4,8,128]{3,0,2,1:T(8,128)(2,1)} %copy.26), calls=%async_computation.1 | async-start | bytes 2097152 | tf_op jit(solution)/shard_map/all_to_all | solution.py:113
  73.3 2.6 %compare_bitcast_fusion = pred[512,2048]{0,1:T(8,128)(4,1)} fusion(s32[4]{0:T(128)S(1)} %copy-done.5, s32[2048]{0:T(1024)S(1)} %get-tuple-element.37, s32[2048]{0:T(1024)S(1)} %get-tuple-element.36, s32[512,4]{0,1:T(4,128)S(1)} %copy-done.4), kind=kOutput, calls=%fused_computation.12 | convolution fusion | flops 9463808 | bytes 1073168 | tf_op jit(solution)/shard_map/while/body/eval_jaxpr/dot_general | solution.py:56
  75.8 22.8 %all-to-all-done = bf16[128,4,8,128]{3,0,2,1:T(8,128)(2,1)S(1)} async-done(((bf16[128,4,8,128]{3,0,2,1:T(8,128)(2,1)}), bf16[128,4,8,128]{3,0,2,1:T(8,128)(2,1)S(1)}, u32[]{:S(2)}, u32[]{:S(2)}) %all-to-all-start) | async-done | bytes 1048608 | tf_op jit(solution)/shard_map/all_to_all | solution.py:113
  98.6 1.1 copy.27
  99.8 2.0 reduce_sum.69
  101.8 0.8 copy.22
  102.7 18.8 %all-gather.5.cloned.1.call-done = bf16[8,256,512]{2,1,0:T(8,128)(2,1)} async-done(((bf16[1,256,512]{2,1,0:T(8,128)(2,1)}), bf16[8,256,512]{2,1,0:T(8,128)(2,1)}) %all-gather.5.cloned.1.call-update) | async-done | bytes 2097168 | tf_op jit(solution)/shard_map/all_gather | solution.py:11
  121.5 2.0 reduce_sum.68
  123.5 0.8 copy.21
  124.3 26.7 %all-gather.9.cloned.1.call-done = bf16[8,256,512]{2,1,0:T(8,128)(2,1)} async-done(((bf16[1,256,512]{2,1,0:T(8,128)(2,1)}), bf16[8,256,512]{2,1,0:T(8,128)(2,1)}) %all-gather.9.cloned.1.call-update) | async-done | bytes 2097168 | tf_op jit(solution)/shard_map/all_gather | solution.py:11
  151.0 2.0 reduce_sum.70
  153.0 0.8 copy.23
  153.8 26.7 %all-gather.11.cloned.1.call-done = bf16[8,256,512]{2,1,0:T(8,128)(2,1)} async-done(((bf16[1,256,512]{2,1,0:T(8,128)(2,1)}), bf16[8,256,512]{2,1,0:T(8,128)(2,1)}) %all-gather.11.cloned.1.call-update) | async-done | bytes 2097168 | tf_op jit(solution)/shard_map/all_gather | solution.py:11
  180.6 2.0 reduce_sum.71
  182.5 0.9 copy.24
  183.4 2.2 pad_maximum_fusion
  185.6 18.3 %fusion.35 = (f32[512,8]{0,1:T(8,128)S(1)}, bf16[512,8,2048]{0,2,1:T(8,128)(2,1)}) fusion(pred[512,2048]{0,1:T(8,128)(4,1)} %compare_bitcast_fusion, bf16[512,8,128]{2,0,1:T(8,128)(2,1)S(1)} %bitcast.66, bf16[256,2048]{0,1:T(8,128)(2,1)} %pad_maximum_fusion), kind=kOutput, calls=%fused_computation.51 | convolution fusion | flops 4353689600 | bytes 22036480 | tf_op jit(solution)/shard_map/while/body/eval_jaxpr/sub | solution.py:63
  203.9 10.8 %fusion.14 = bf16[512,1,8,128]{3,0,2,1:T(8,128)(2,1)S(1)} fusion(bf16[512,8,2048]{0,2,1:T(8,128)(2,1)} %get-tuple-element.35, f32[512,8]{0,1:T(8,128)S(1)} %broadcast_maximum_fusion, bf16[256,2048]{0,1:T(8,128)(2,1)} %pad_maximum_fusion), kind=kOutput, calls=%fused_computation.15 | convolution fusion | flops 2148532224 | bytes 18366464 | tf_op jit(solution)/shard_map/while/body/eval_jaxpr/rnk,dk->rnd/dot_general | solution.py:65
  214.7 0.7 copy.30
  215.4 30.5 %all_to_all.30 = bf16[512,1,8,128]{3,2,1,0:T(8,128)(2,1)S(1)} all-to-all(bf16[512,1,8,128]{3,2,1,0:T(8,128)(2,1)S(1)} %copy.30), channel_id=1, replica_groups=mesh['ctx'=8,'head'=4] {'head'}, dimensions={0} | all-to-all | bytes 2097152 | tf_op jit(solution)/shard_map/all_to_all | solution.py:119
  246.1 1.3 reshape.183
  (25 shorter events, 1.5 us)
Async XLA Ops:
  6.5 1.6 copy-start
  6.5 7.6 %copy-start.2 = (s32[4]{0:T(128)S(1)}, s32[4]{0:T(128)}, u32[]{:S(2)}) copy-start(s32[4]{0:T(128)} %param.13) | copy-start | bytes 52
  6.5 56.0 %copy-start.3 = (f32[128]{0:T(128)S(1)}, f32[128]{0:T(128)}, u32[]{:S(2)}) copy-start(f32[128]{0:T(128)} %param.10) | copy-start | bytes 1540
  6.5 54.0 %reduce-scatter.2.cloned.1.call-start = ((), (), s32[]{:S(2)}) async-start(), calls=%async_computation.3 | async-start | bytes 2621440 | tf_op jit(solution)/shard_map/reduce_scatter | solution.py:86
  14.1 85.7 %all-gather.7.cloned.1.call-start = ((), (), s32[]{:S(2)}) async-start(), calls=%async_computation.5 | async-start | bytes 2359296 | tf_op jit(solution)/shard_map/all_gather | solution.py:11
  63.6 9.7 %copy-start.4 = (s32[512,4]{0,1:T(4,128)S(1)}, s32[512,4]{0,1:T(4,128)}, u32[]{:S(2)}) copy-start(s32[512,4]{0,1:T(4,128)} %param.11) | copy-start | bytes 24580
  63.6 9.7 %copy-start.5 = (s32[4]{0:T(128)S(1)}, s32[4]{0:T(128)}, u32[]{:S(2)}) copy-start(s32[4]{0:T(128)} %param.12) | copy-start | bytes 52
  64.6 56.9 %all-gather.5.cloned.1.call-start = ((), (), s32[]{:S(2)}) async-start(), calls=%async_computation.4 | async-start | bytes 2359296 | tf_op jit(solution)/shard_map/all_gather | solution.py:11
  65.4 85.7 %all-gather.9.cloned.1.call-start = ((), (), s32[]{:S(2)}) async-start(), calls=%async_computation.6 | async-start | bytes 2359296 | tf_op jit(solution)/shard_map/all_gather | solution.py:11
  65.9 114.6 %all-gather.11.cloned.1.call-start = ((), (), s32[]{:S(2)}) async-start(), calls=%async_computation.7 | async-start | bytes 2359296 | tf_op jit(solution)/shard_map/all_gather | solution.py:11
  69.5 29.1 %all-to-all-start = ((bf16[128,4,8,128]{3,0,2,1:T(8,128)(2,1)}), bf16[128,4,8,128]{3,0,2,1:T(8,128)(2,1)S(1)}, u32[]{:S(2)}, u32[]{:S(2)}) async-start(bf16[128,4,8,128]{3,0,2,1:T(8,128)(2,1)} %copy.26), calls=%async_computation.1 | async-start | bytes 2097152 | tf_op jit(solution)/shard_map/all_to_all | solution.py:113
  123.4 62.2 %copy-start.1 = (bf16[4,128,1,8,128]{4,1,0,3,2:T(8,128)(2,1)S(1)}, bf16[4,128,1,8,128]{4,1,0,3,2:T(8,128)(2,1)}, u32[]{:S(2)}) copy-start(bf16[4,128,1,8,128]{4,1,0,3,2:T(8,128)(2,1)} %copy.27) | copy-start | bytes 3145732
Sparse Core Ops, SparseCore 0:
  14.2 46.3 reduce-scatter.1
  64.7 26.9 all-gather.6
  93.7 27.7 all-gather.4
  123.2 27.7 all-gather.8
  152.8 27.7 all-gather.10
